TPU v7x, 32 devices: a whole 2x2x4 slice. The times are simulated.
32 devices in a mesh: tm: 4 (over x, core), chan: 8 (over z, y).
Axes of the slice: x: 2, y: 2, z: 4, core: 2. Of those that a mesh axis runs over, the one named last changes fastest.
Arguments:
- raw_blocks: bfloat16 [16, 5120, 1024], P('tm', 'chan'), may hold values from -6 to 6
- fir_taps: bfloat16 [128], replicated, may hold values from -0.5 to 0.5
- recorder_channel: int32 [5120], replicated, may hold values from 0 to 5119, as said below
- pairs: int32 [4096, 2], P('chan'), may hold values from 0 to 5119, as said below
Outputs:
- stacks: float32 [4096, 256], P('chan')
Inputs may be any that keep to these rules, and one draw needn't show every extreme that they name: `recorder_channel`: A permutation of the channels; each aligned block of 640 recorder rows holds exactly 80 channels of every range of 640 consecutive channels. `pairs`: each aligned block of 512 rows names exactly 32 distinct channels of every range of 640 consecutive channels.
All inputs are finite; a program needn't handle non-finite values.
Results may differ from a plain program's by a relative error of at most 0.0084.
Values may be sent and summed in bfloat16 or wider, within the bound.
No kernel may reach another device: no remote copies, remote signals or barrier semaphores. Data moves between devices by JAX's collectives and lax.ppermute only.
A program may use at most 128 MiB of HBM per device.

v0:
```python
import jax
import jax.numpy as jnp
from jax import lax
from jax.sharding import PartitionSpec as P

NB = 128
SMOOTH = 4


def make_fir(fir_taps, length):
    taps_n = fir_taps.shape[0]
    period = taps_n + length
    padded = jnp.concatenate([fir_taps.astype(jnp.float32), jnp.zeros((length,), jnp.float32)])
    repeated = jnp.tile(padded, length)[: length * (period - 1)].reshape(length, period - 1)[
        :, :length
    ]
    return repeated.astype(jnp.bfloat16)


def make_table(length, bin_count):
    samples = jnp.arange(length, dtype=jnp.int32)
    freqs = jnp.arange(1, bin_count + 1, dtype=jnp.int32)
    phase_idx = samples[:, None] * freqs[None, :] % length
    angles = phase_idx.astype(jnp.float32) * (2.0 * jnp.pi / length)
    return jnp.concatenate([jnp.cos(angles), -jnp.sin(angles)], axis=1).astype(jnp.bfloat16)


def make_smooth(bin_count, half_width):
    places = jnp.arange(bin_count, dtype=jnp.int32)
    band_mask = (jnp.abs(places[:, None] - places[None, :]) <= half_width).astype(jnp.float32)
    return band_mask / jnp.sum(band_mask, axis=0, keepdims=True)


def whiten(spectrum, smoother):
    bin_count = spectrum.shape[-1] // 2
    real_part = spectrum[..., :bin_count]
    imag_part = spectrum[..., bin_count:]
    magnitude = jnp.sqrt(real_part * real_part + imag_part * imag_part)
    smoothed = jnp.dot(magnitude, smoother, precision=lax.Precision.HIGHEST)
    mean_level = jnp.mean(magnitude, axis=-1, keepdims=True)
    divisor = smoothed + 0.1 * mean_level + 1e-06
    return (spectrum / jnp.concatenate([divisor, divisor], axis=-1)).astype(jnp.bfloat16)


def cross(left_rows, right_rows):
    bin_count = left_rows.shape[-1] // 2
    left_f = left_rows.astype(jnp.float32)
    right_f = right_rows.astype(jnp.float32)
    left_re, left_im = (left_f[..., :bin_count], left_f[..., bin_count:])
    right_re, right_im = (right_f[..., :bin_count], right_f[..., bin_count:])
    real_out = left_re * right_re + left_im * right_im
    imag_out = left_im * right_re - left_re * right_im
    return jnp.concatenate([real_out, imag_out], axis=-1)


def local(raw_blocks, fir_taps, recorder_channel, pairs):
    windows, ch_dev, length = raw_blocks.shape
    rows_of = jnp.argsort(recorder_channel, stable=True)
    endpoints = jnp.concatenate([pairs[:, 0], pairs[:, 1]])
    wanted_ids = jnp.take(rows_of, endpoints)
    fir_matrix = make_fir(fir_taps, length)
    dft_table = make_table(length, NB)
    smoother = make_smooth(NB, SMOOTH)
    flat_rows = raw_blocks.reshape(windows * ch_dev, length)
    filtered = jnp.dot(flat_rows, fir_matrix, preferred_element_type=jnp.float32).astype(
        jnp.bfloat16
    )
    spectrum = jnp.dot(filtered, dft_table, preferred_element_type=jnp.float32)
    whitened = whiten(spectrum, smoother).reshape(windows, ch_dev, 2 * NB)
    pair_count = pairs.shape[0]
    empty = jnp.zeros((windows, 2 * pair_count, 2 * NB), jnp.bfloat16)
    part_rows = lax.all_gather(whitened, "chan", axis=1, tiled=True)
    inside = (wanted_ids >= 0) & (wanted_ids < part_rows.shape[1])
    taken = jnp.take(part_rows, jnp.clip(wanted_ids, 0, part_rows.shape[1] - 1), axis=1)
    chosen = jnp.where(inside[None, :, None], taken, empty)
    products = cross(chosen[:, :pair_count], chosen[:, pair_count:])
    stacked = jnp.sum(products, axis=0)
    summed = lax.psum(stacked, "tm")
    return summed / (windows * lax.axis_size("tm"))


def solution(mesh):
    in_specs = (P("tm", "chan", None), P(), P(), P("chan", None))
    out_specs = P("chan", None)
    return jax.shard_map(local, mesh=mesh, in_specs=in_specs, out_specs=out_specs, check_vma=False)
```

profile of v0, /device:TPU:0, one launch (start us, length us, event | category | flops | bytes accessed | tf_op | source)
XLA Modules:
  0.0 248.1 jit_solution(11060469899976761753)
XLA Ops:
  6.5 0.0 all-gather.2.cloned.1.call-start
  6.6 2.2 cosine_convert_fusion
  8.8 0.7 concatenate.69
  9.5 0.2 tile.10
  9.7 3.8 %tile.11 = bf16[1179648]{0:T(1024)(128)(2,1)} reshape(bf16[1024,1152]{1,0:T(8,128)(2,1)S(1)} %tile.10) | data formatting | bytes 4718592 | tf_op jit(solution)/shard_map/tile | solution.py:14
  13.5 0.0 slice-start
  13.5 1.7 slice-done
  15.2 6.4 %reshape.232 = bf16[1024,1151]{1,0:T(8,128)(2,1)} reshape(bf16[1178624]{0:T(1024)(128)(2,1)S(1)} %slice-done) | data formatting | bytes 4714496 | tf_op jit(solution)/shard_map/reshape | solution.py:14
  21.5 10.3 %fusion.6 = f32[2560,256]{1,0:T(8,128)S(1)} fusion(bf16[2560,1024]{1,0:T(8,128)(2,1)} %bitcast.16, bf16[1024,1151]{1,0:T(8,128)(2,1)} %reshape.232, bf16[1024,128]{1,0:T(8,128)(2,1)S(1)} %get-tuple-element.16, bf16[1024,128]{1,0:T(8,128)(2,1)S(1)} %get-tuple-element.15), kind=kOutput, calls=%fused_computation.14 | convolution fusion | flops 6714556416 | bytes 10485760 | tf_op jit(solution)/shard_map/dot_general | solution.py:68
  31.9 0.5 fusion.17
  32.4 1.5 fusion
  33.9 0.5 fusion.1
  34.4 0.0 copy-start
  34.5 0.0 copy-start.1
  34.5 2.1 copy.11
  36.6 0.0 all-gather.2.cloned.1.call-update
  36.6 0.0 all-reduce.3.cloned.1.call-start
  36.6 0.0 copy-done
  36.6 6.8 %sort.17 = (s32[5120]{0:T(1024)}, s32[5120]{0:T(1024)S(1)}) sort(s32[5120]{0:T(1024)S(1)} %copy-done, s32[5120]{0:T(1024)S(1)} %iota.22), dimensions={0}, to_apply=%region_0.0 | sort | flops 66560 | bytes 81920 | tf_op jit(solution)/shard_map/jit(argsort)/sort | solution.py:58
  43.4 0.0 copy-done.1
  43.4 6.4 %gather_fusion = s32[1024]{0:T(1024)S(1)} fusion(s32[5120]{0:T(1024)S(1)} %get-tuple-element.6, s32[1024]{0:T(1024)S(1)} %broadcast_clamp_fusion.1), kind=kCustom, calls=%fused_computation | custom fusion | bytes 12288 | tf_op jit(solution)/shard_map/jit(_take)/gather | solution.py:60
  49.9 140.1 %all-gather.2.cloned.1.call-done = bf16[4,5120,256]{2,0,1:T(4,128)(2,1)} async-done(((bf16[4,640,256]{2,0,1:T(4,128)(2,1)}), bf16[4,5120,256]{2,0,1:T(4,128)(2,1)}) %all-gather.2.cloned.1.call-update) | async-done | bytes 10485776 | tf_op jit(solution)/shard_map/all_gather | solution.py:72
  190.0 7.9 %gather_fusion.1 = bf16[1024,4,256]{2,1,0:T(4,128)(2,1)S(1)} fusion(bf16[4,5120,256]{2,0,1:T(4,128)(2,1)} %all-gather.2.cloned.1.call-done, s32[1024]{0:T(1024)S(1)} %broadcast_clamp_fusion), kind=kCustom, calls=%fused_computation.1 | custom fusion | bytes 4198400 | tf_op jit(solution)/shard_map/jit(_take)/gather | solution.py:74
  197.9 6.5 %select_bitcast_fusion = bf16[4,1024,256]{2,0,1:T(4,128)(2,1)S(1)} fusion(bf16[1024,4,256]{2,1,0:T(4,128)(2,1)S(1)} %gather_fusion.1, pred[1024]{0:T(1024)(128)(4,1)S(1)} %get-tuple-element.12, pred[1024]{0:T(1024)(128)(4,1)S(1)} %get-tuple-element.11), kind=kLoop, calls=%fused_computation.9 | loop fusion | flops 2097152 | bytes 4196352 | tf_op jit(solution)/shard_map/jit(_where)/select_n | solution.py:75
  204.4 0.5 slice_convert_fusion.1
  204.9 0.5 multiply_add_fusion
  205.5 2.2 maximum_reduce_fusion
  207.7 0.0 all-reduce.3.cloned.1.call-update
  207.7 31.7 %all-reduce.3.cloned.1.call-done = f32[512,256]{1,0:T(8,128)} async-done(((f32[512,256]{1,0:T(8,128)}), f32[512,256]{1,0:T(8,128)}) %all-reduce.3.cloned.1.call-update) | async-done | bytes 524304 | tf_op jit(solution)/shard_map/psum | solution.py:78
  239.4 1.9 broadcast_multiply_fusion
  (10 shorter events, 0.1 us)
Async XLA Ops:
  6.5 183.4 %all-gather.2.cloned.1.call-start = ((), (), s32[]{:S(2)}) async-start(), calls=%async_computation | async-start | bytes 11796480 | tf_op jit(solution)/shard_map/all_gather | solution.py:72
  13.5 1.7 slice-start
  34.4 2.2 copy-start
  34.5 9.0 %copy-start.1 = (s32[512,2]{0,1:T(2,128)S(1)}, s32[512,2]{0,1:T(2,128)}, u32[]{:S(2)}) copy-start(s32[512,2]{0,1:T(2,128)} %param.7) | copy-start | bytes 12292
  36.6 202.8 %all-reduce.3.cloned.1.call-start = ((), (), s32[]{:S(2)}) async-start(), calls=%async_computation.1 | async-start | bytes 1048576 | tf_op jit(solution)/shard_map/psum | solution.py:78
Sparse Core Ops, SparseCore 0:
  36.7 153.2 all-gather.1
  207.8 31.5 all-reduce.2
where the time goes:
time: 248 us
  waiting for transfers between devices  172 us (69%)
  local copies, waits for them, and re-layouts  29.1 us (12%)
  other arithmetic  21.8 us (9%)
  between operations  13.5 us (5%)
  matrix products  11.8 us (5%)
    all_gather x1, waiting for transfers between devices, local(): part_rows = lax.all_gather(whitened, 'chan', axis=1, tiled=True)  140 us
    psum x1, waiting for transfers between devices, local(): summed = lax.psum(stacked, 'tm')  31.7 us
    dot_general x1, matrix products, local(): spectrum = jnp.dot(filtered, dft_table, preferred_element_type=jnp.float32)  10.3 us
    gather x1, local copies, waits for them, and re-layouts, local(): jnp.take(part_rows, jnp.clip(wanted_ids, 0, part_rows.shape[1] - 1), axis=1)  7.92 us
    sort x1, other arithmetic, local(): rows_of = jnp.argsort(recorder_channel, stable=True)  6.76 us
    select_n x1, other arithmetic, local(): chosen = jnp.where(inside[None, :, None], taken, empty)  6.46 us
    gather x1, local copies, waits for them, and re-layouts, local(): wanted_ids = jnp.take(rows_of, endpoints)  6.37 us
    reshape x1, local copies, waits for them, and re-layouts, make_fir(): jnp.tile(padded, length)[:length * (period - 1)].reshape(length, period - 1)  6.35 us
  transfers between devices with their start and end apart: 2, of which 2 were waited for; matrix products, arithmetic and copies ran while one was open for 5% of the time, Pallas kernels for 0%

commit v1 on v0

--- a/solution.py
+++ b/solution.py
@@ -69,7 +69,7 @@
     whitened = whiten(spectrum, smoother).reshape(windows, ch_dev, 2 * NB)
     pair_count = pairs.shape[0]
     empty = jnp.zeros((windows, 2 * pair_count, 2 * NB), jnp.bfloat16)
-    part_rows = lax.all_gather(whitened, "chan", axis=1, tiled=True)
+    part_rows = jnp.concatenate(lax.all_gather(whitened, "chan"), axis=1)
     inside = (wanted_ids >= 0) & (wanted_ids < part_rows.shape[1])
     taken = jnp.take(part_rows, jnp.clip(wanted_ids, 0, part_rows.shape[1] - 1), axis=1)
     chosen = jnp.where(inside[None, :, None], taken, empty)

time: 248 us -> 262 us (1.056)
  local copies, waits for them, and re-layouts: 29.1 us -> 41.4 us
    reshape x1, local copies, waits for them, and re-layouts: 2.09 us -> 14.6 us  [local(): part_rows = jnp.concatenate(lax.all_gather(whitened, 'chan'), axis=1)]
where the time goes in v1:
time: 262 us
  waiting for transfers between devices  172 us (66%)
  local copies, waits for them, and re-layouts  41.4 us (16%)
  other arithmetic  23 us (9%)
  between operations  13.5 us (5%)
  matrix products  11.7 us (4%)
    all_gather x1, waiting for transfers between devices, local(): part_rows = jnp.concatenate(lax.all_gather(whitened, 'chan'), axis=1)  140 us
    psum x1, waiting for transfers between devices, local(): summed = lax.psum(stacked, 'tm')  31.7 us
    reshape x1, local copies, waits for them, and re-layouts, local(): part_rows = jnp.concatenate(lax.all_gather(whitened, 'chan'), axis=1)  14.6 us
    dot_general x1, matrix products, local(): spectrum = jnp.dot(filtered, dft_table, preferred_element_type=jnp.float32)  10.2 us
    gather x1, local copies, waits for them, and re-layouts, local(): jnp.take(part_rows, jnp.clip(wanted_ids, 0, part_rows.shape[1] - 1), axis=1)  7.92 us
    sort x1, other arithmetic, local(): rows_of = jnp.argsort(recorder_channel, stable=True)  6.76 us
    select_n x1, other arithmetic, local(): chosen = jnp.where(inside[None, :, None], taken, empty)  6.46 us
    reshape x1, local copies, waits for them, and re-layouts, make_fir(): jnp.tile(padded, length)[:length * (period - 1)].reshape(length, period - 1)  6.35 us
  transfers between devices with their start and end apart: 2, of which 2 were waited for; matrix products, arithmetic and copies ran while one was open for 5% of the time, Pallas kernels for 0%

profile of v1, /device:TPU:0, one launch (start us, length us, event | category | flops | bytes accessed | tf_op | source)
XLA Modules:
  0.0 261.7 jit_solution(6801155272109285621)
XLA Ops:
  6.5 0.0 all-gather.2.cloned.1.call-start
  6.6 0.7 concatenate.69
  7.2 0.2 tile.10
  7.4 3.8 %tile.11 = bf16[1179648]{0:T(1024)(128)(2,1)} reshape(bf16[1024,1152]{1,0:T(8,128)(2,1)S(1)} %tile.10) | data formatting | bytes 4718592 | tf_op jit(solution)/shard_map/tile | solution.py:14
  11.3 0.0 slice-start
  11.3 1.7 slice-done
  12.9 6.4 %reshape.235 = bf16[1024,1151]{1,0:T(8,128)(2,1)} reshape(bf16[1178624]{0:T(1024)(128)(2,1)S(1)} %slice-done) | data formatting | bytes 4714496 | tf_op jit(solution)/shard_map/reshape | solution.py:14
  19.3 2.4 cosine_convert_fusion
  21.7 10.2 %fusion.6 = f32[2560,256]{1,0:T(8,128)S(1)} fusion(bf16[2560,1024]{1,0:T(8,128)(2,1)} %bitcast.22, bf16[1024,1151]{1,0:T(8,128)(2,1)} %reshape.235, bf16[1024,128]{1,0:T(8,128)(2,1)S(1)} %get-tuple-element.16, bf16[1024,128]{1,0:T(8,128)(2,1)S(1)} %get-tuple-element.15), kind=kOutput, calls=%fused_computation.14 | convolution fusion | flops 6714556416 | bytes 10485760 | tf_op jit(solution)/shard_map/dot_general | solution.py:68
  31.8 0.5 fusion.17
  32.4 1.5 fusion
  33.9 0.0 copy-start
  33.9 0.0 copy-start.1
  33.9 1.6 fusion.1
  35.5 0.0 all-gather.2.cloned.1.call-update
  35.5 0.3 all-reduce.3.cloned.1.call-start
  35.8 0.0 copy-done
  35.8 6.8 %sort.17 = (s32[5120]{0:T(1024)}, s32[5120]{0:T(1024)S(1)}) sort(s32[5120]{0:T(1024)S(1)} %copy-done, s32[5120]{0:T(1024)S(1)} %iota.22), dimensions={0}, to_apply=%region_0.0 | sort | flops 66560 | bytes 81920 | tf_op jit(solution)/shard_map/jit(argsort)/sort | solution.py:58
  42.6 0.0 copy-done.1
  42.6 6.2 %gather_fusion = s32[1024]{0:T(1024)S(1)} fusion(s32[5120]{0:T(1024)S(1)} %get-tuple-element.6, s32[1024]{0:T(1024)S(1)} %broadcast_clamp_fusion.1), kind=kCustom, calls=%fused_computation | custom fusion | bytes 12288 | tf_op jit(solution)/shard_map/jit(_take)/gather | solution.py:60
  48.8 140.1 %all-gather.2.cloned.1.call-done = bf16[8,4,640,256]{3,2,0,1:T(8,128)(2,1)} async-done(((bf16[1,4,640,256]{3,2,0,1:T(8,128)(2,1)}), bf16[8,4,640,256]{3,2,0,1:T(8,128)(2,1)}) %all-gather.2.cloned.1.call-update) | async-done | bytes 10485776 | tf_op jit(solution)/shard_map/all_gather | solution.py:72
  188.9 14.6 %copy.11 = bf16[4,5120,256]{2,0,1:T(4,128)(2,1)} copy(bf16[4,5120,256]{2,1,0:T(8,128)(2,1)} %bitcast.15) | data formatting | bytes 20971520 | tf_op jit(solution)/shard_map/reshape | solution.py:72
  203.6 7.9 %gather_fusion.1 = bf16[1024,4,256]{2,1,0:T(4,128)(2,1)S(1)} fusion(bf16[4,5120,256]{2,0,1:T(4,128)(2,1)} %copy.11, s32[1024]{0:T(1024)S(1)} %broadcast_clamp_fusion), kind=kCustom, calls=%fused_computation.1 | custom fusion | bytes 4198400 | tf_op jit(solution)/shard_map/jit(_take)/gather | solution.py:74
  211.5 6.5 %select_bitcast_fusion = bf16[4,1024,256]{2,0,1:T(4,128)(2,1)S(1)} fusion(bf16[1024,4,256]{2,1,0:T(4,128)(2,1)S(1)} %gather_fusion.1, pred[1024]{0:T(1024)(128)(4,1)S(1)} %get-tuple-element.12, pred[1024]{0:T(1024)(128)(4,1)S(1)} %get-tuple-element.11), kind=kLoop, calls=%fused_computation.9 | loop fusion | flops 2097152 | bytes 4196352 | tf_op jit(solution)/shard_map/jit(_where)/select_n | solution.py:75
  217.9 0.5 slice_convert_fusion.1
  218.5 0.5 multiply_add_fusion
  219.0 2.2 maximum_reduce_fusion
  221.2 0.0 all-reduce.3.cloned.1.call-update
  221.3 31.7 %all-reduce.3.cloned.1.call-done = f32[512,256]{1,0:T(8,128)} async-done(((f32[512,256]{1,0:T(8,128)}), f32[512,256]{1,0:T(8,128)}) %all-reduce.3.cloned.1.call-update) | async-done | bytes 524304 | tf_op jit(solution)/shard_map/psum | solution.py:78
  253.0 1.9 broadcast_multiply_fusion
  (10 shorter events, 0.1 us)
Async XLA Ops:
  6.5 182.4 %all-gather.2.cloned.1.call-start = ((), (), s32[]{:S(2)}) async-start(), calls=%async_computation | async-start | bytes 11796480 | tf_op jit(solution)/shard_map/all_gather | solution.py:72
  11.3 1.7 slice-start
  33.9 1.9 copy-start
  33.9 8.6 %copy-start.1 = (s32[512,2]{0,1:T(2,128)S(1)}, s32[512,2]{0,1:T(2,128)}, u32[]{:S(2)}) copy-start(s32[512,2]{0,1:T(2,128)} %param.7) | copy-start | bytes 12292
  35.5 217.5 %all-reduce.3.cloned.1.call-start = ((), (), s32[]{:S(2)}) async-start(), calls=%async_computation.1 | async-start | bytes 1048576 | tf_op jit(solution)/shard_map/psum | solution.py:78
Sparse Core Ops, SparseCore 0:
  35.6 153.2 all-gather.1
  221.4 31.5 all-reduce.2
